TPU v7x, 256 devices: a whole 4x4x8 slice. The times are simulated.
256 devices in a mesh: dom: 32 (over x, y, core), tm: 8 (over z).
Axes of the slice: x: 4, y: 4, z: 8, core: 2. Of those that a mesh axis runs over, the one named last changes fastest.
Arguments:
- features: bfloat16 [8, 8192, 512], P('tm', 'dom'), may hold values from -6 to 6
- tile_rows: int32 [8, 768], P('tm', 'dom'), may hold values from 0 to 63, as said below
- tile_cols: int32 [8, 768], P('tm', 'dom'), may hold values from 0 to 63, as said below
- tile_vals: bfloat16 [8, 768, 128, 128], P('tm', 'dom'), may hold values from 0 to 0.0625
- tile_used: int32 [8, 32], P('tm', 'dom'), may hold values from 12 to 24, as said below
- pool_weight: bfloat16 [512, 512], replicated, may hold values from -0.25 to 0.25
- w_in: bfloat16 [3, 512, 512], replicated, may hold values from -0.25 to 0.25
- w_state: bfloat16 [3, 512, 512], replicated, may hold values from -0.25 to 0.25
- gate_offset: float32 [512], replicated, may hold values from 0 to 5
- start_weight: float32 [512, 512], replicated, may hold values from -3 to 3
Outputs:
- hidden_out: bfloat16 [8, 8192, 512], P('tm', 'dom')
- weights_out: float32 [8, 512, 512], P('tm')
Inputs may be any that keep to these rules, and one draw needn't show every extreme that they name: `tile_rows`: every slot of row partition d names a row block of that partition, d * 2 to (d + 1) * 2 - 1. `tile_cols`: within one snapshot and one row partition, all slots whose column blocks lie on the same dom index name the same column block. `tile_used`: in every snapshot some row partition has all 24 slots live.
All inputs are finite; a program needn't handle non-finite values.
Results may differ from a plain program's by a relative error of at most 0.017.
Values may be sent and summed in bfloat16 or wider, within the bound.
No kernel may reach another device: no remote copies, remote signals or barrier semaphores. Data moves between devices by JAX's collectives and lax.ppermute only.
A program may use at most 64 MiB of HBM per device.

v0:
```python
import jax
import jax.numpy as jnp
from jax import lax
from jax.sharding import PartitionSpec as P

BLOCK = 128


def shifted(block, axis, distance):
    devices = range(lax.axis_size(axis))
    route = [(i - distance, i) for i in devices if i - distance in devices]
    return lax.ppermute(block, axis, route)


def gru_step(state, inputs_t, w_state, gate_offset):
    state_b = state.astype(jnp.bfloat16)
    upd_pre = jnp.dot(w_state[0], state_b, preferred_element_type=jnp.float32)
    rst_pre = jnp.dot(w_state[1], state_b, preferred_element_type=jnp.float32)
    update = jax.nn.sigmoid(inputs_t[0] + upd_pre - gate_offset[:, None])
    reset = jax.nn.sigmoid(inputs_t[1] + rst_pre)
    reset_state = (reset * state).astype(jnp.bfloat16)
    candidate = jnp.tanh(
        inputs_t[2] + jnp.dot(w_state[2], reset_state, preferred_element_type=jnp.float32)
    )
    return (1.0 - update) * state + update * candidate


def shards(
    features,
    tile_rows,
    tile_cols,
    tile_vals,
    tile_used,
    pool_weight,
    w_in,
    w_state,
    gate_offset,
    start_weight,
):
    snap_dev, rows_dev, width = features.shape
    slots = tile_rows.shape[1]
    n_dom = lax.axis_size("dom")
    n_tm = lax.axis_size("tm")
    dom_index = lax.axis_index("dom")
    tm_index = lax.axis_index("tm")
    blocks_dev = rows_dev // BLOCK
    local_rows = tile_rows - dom_index * blocks_dev
    owner_dev = tile_cols // blocks_dev
    block_pick = tile_cols % blocks_dev
    live_mask = jnp.arange(slots, dtype=jnp.int32)[None, :] < tile_used
    peer_ids = jnp.arange(n_dom, dtype=jnp.int32)
    matches = (owner_dev[:, None, :] == peer_ids[None, :, None]) & live_mask[:, None, :]
    wanted_block = jnp.max(jnp.where(matches, block_pick[:, None, :], 0), axis=2)
    snap_base = (jnp.arange(snap_dev, dtype=jnp.int32) * blocks_dev)[:, None]
    wanted = (wanted_block + snap_base).T
    flat_blocks = features.reshape(snap_dev * blocks_dev, BLOCK, width)
    replies = jnp.take(
        flat_blocks, lax.all_to_all(wanted, "dom", split_axis=0, concat_axis=0, tiled=True), axis=0
    )
    fetched = lax.all_to_all(replies, "dom", split_axis=0, concat_axis=0, tiled=True)

    def source_of(s, j):
        return fetched[owner_dev[s, j], s]

    s = 0
    totals = features[s].astype(jnp.float32).reshape(blocks_dev, BLOCK, width)

    def add_tile(j, totals, s=s):
        product = jnp.dot(tile_vals[s, j], source_of(s, j), preferred_element_type=jnp.float32)
        return totals.at[local_rows[s, j]].add(product)

    totals = lax.fori_loop(0, tile_used[s, 0], add_tile, totals)
    aggregated = [totals.reshape(rows_dev, width).astype(jnp.bfloat16)]
    s = 0
    pool_gates = jax.nn.sigmoid(
        jnp.dot(features[s], pool_weight, preferred_element_type=jnp.float32)
    ).astype(jnp.bfloat16)
    partial_pool = [
        jnp.einsum("nd,nk->dk", features[s], pool_gates, preferred_element_type=jnp.float32)
    ]
    pooled = lax.psum(jnp.stack(partial_pool).astype(jnp.bfloat16), "dom").astype(jnp.float32)
    summary = (pooled * (rows_dev * n_dom) ** (-0.5)).astype(jnp.bfloat16)
    in_side = jnp.einsum("gij,tjk->tgik", w_in, summary, preferred_element_type=jnp.float32)

    def run_final(state):
        state = gru_step(state, in_side[0], w_state, gate_offset)
        return state

    def keep_state(state):
        return state

    state = start_weight
    for k in range(n_tm - 1):
        final = lax.cond(tm_index == k, run_final, keep_state, state)
        incoming = shifted(final.astype(jnp.bfloat16), "tm", 1).astype(final.dtype)
        state = jnp.where(tm_index == k + 1, incoming, state)
    s = 0
    state = gru_step(state, in_side[s], w_state, gate_offset)
    history = [state]
    evolved = jnp.stack(history)
    s = 0
    mixed = jnp.dot(
        aggregated[s], evolved[s].astype(jnp.bfloat16), preferred_element_type=jnp.float32
    )
    outputs = [jnp.maximum(mixed * width ** (-0.5), 0.0).astype(jnp.bfloat16)]
    return (jnp.stack(outputs), evolved)


def solution(mesh):
    in_specs = (
        P("tm", "dom", None),
        P("tm", "dom"),
        P("tm", "dom"),
        P("tm", "dom", None, None),
        P("tm", "dom"),
        P(),
        P(),
        P(),
        P(),
        P(),
    )
    out_specs = (P("tm", "dom", None), P("tm", None, None))
    return jax.shard_map(shards, mesh=mesh, in_specs=in_specs, out_specs=out_specs, check_vma=False)
```

profile of v0, /device:TPU:162, one launch (start us, length us, event | category | flops | bytes accessed | tf_op | source)
XLA Modules:
  0.0 496.8 jit_solution(9960098003639466256)
XLA Ops:
  7.2 2.8 fusion.220
  10.1 116.7 %all-reduce.2.cloned.1.call-done = bf16[1,512,512]{1,2,0:T(8,128)(2,1)} async-done(((bf16[1,512,512]{1,2,0:T(8,128)(2,1)}), bf16[1,512,512]{1,2,0:T(8,128)(2,1)}) %all-reduce.2.cloned.1.call-update) | async-done | bytes 524304 | tf_op jit(solution)/shard_map/psum | solution.py:81
  126.8 3.7 convolution_bitcast_fusion.8
  130.8 2.6 collective-permute-start
  135.3 11.3 %collective-permute-done = bf16[512,512]{0,1:T(8,128)(2,1)S(1)} collective-permute-done((bf16[512,512]{0,1:T(8,128)(2,1)S(1)}, bf16[512,512]{0,1:T(8,128)(2,1)S(1)}, u32[]{:S(2)}, u32[]{:S(2)}) %collective-permute-start) | collective-permute-done | bytes 524320 | tf_op jit(solution)/shard_map/ppermute | solution.py:12
  148.5 2.6 collective-permute-start.1
  151.9 6.2 %all-to-all-start = ((s32[32,1,1]{2,1,0:T(1,128)}), s32[32,1,1]{2,1,0:T(1,128)S(1)}, u32[]{:S(2)}, u32[]{:S(2)}) async-start(s32[32,1,1]{2,1,0:T(1,128)} %copy.126), calls=%async_computation | async-start | bytes 32768 | tf_op jit(solution)/shard_map/all_to_all | solution.py:58
  158.2 6.1 %all-to-all-done = s32[32,1,1]{2,1,0:T(1,128)S(1)} async-done(((s32[32,1,1]{2,1,0:T(1,128)}), s32[32,1,1]{2,1,0:T(1,128)S(1)}, u32[]{:S(2)}, u32[]{:S(2)}) %all-to-all-start) | async-done | bytes 160 | tf_op jit(solution)/shard_map/all_to_all | solution.py:58
  166.2 2.6 collective-permute-start.2
  168.8 2.8 gather_fusion
  171.7 4.7 bitcast_select_fusion
  176.3 6.1 %all-to-all-start.1 = ((bf16[32,1,128,512]{3,2,1,0:T(8,128)(2,1)}), bf16[32,1,128,512]{3,2,1,0:T(8,128)(2,1)}, u32[]{:S(2)}, u32[]{:S(2)}) async-start(bf16[32,1,128,512]{3,2,1,0:T(8,128)(2,1)} %bitcast_select_fusion), calls=%async_computation.1 | async-start | bytes 8388608 | tf_op jit(solution)/shard_map/all_to_all | solution.py:60
  183.1 1.9 collective-permute-start.3
  185.0 14.1 %collective-permute-done.3 = bf16[512,512]{0,1:T(8,128)(2,1)S(1)} collective-permute-done((bf16[512,512]{0,1:T(8,128)(2,1)S(1)}, bf16[512,512]{0,1:T(8,128)(2,1)S(1)}, u32[]{:S(2)}, u32[]{:S(2)}) %collective-permute-start.3) | collective-permute-done | bytes 524320 | tf_op jit(solution)/shard_map/ppermute | solution.py:12
  199.7 2.0 collective-permute-start.4
  201.7 51.7 %collective-permute-done.4 = bf16[512,512]{0,1:T(8,128)(2,1)S(1)} collective-permute-done((bf16[512,512]{0,1:T(8,128)(2,1)S(1)}, bf16[512,512]{0,1:T(8,128)(2,1)S(1)}, u32[]{:S(2)}, u32[]{:S(2)}) %collective-permute-start.4) | collective-permute-done | bytes 524320 | tf_op jit(solution)/shard_map/ppermute | solution.py:12
  253.6 10.0 %conditional.12 = (bf16[512,512]{1,0:T(8,128)(2,1)S(1)}) conditional(s32[]{:T(128)} %convert_element_type.155, (f32[512,512]{0,1:T(8,128)S(1)}) %tuple.103, (f32[1,3,512,512]{2,3,1,0:T(8,128)}, bf16[3,512,512]{2,1,0:T(8,128)(2,1)}, f32[512,512]{0,1:T(8,128)S(1)}, f32[512]{0:T(512)S(1)}) %tuple.144), branch_computations={%region_15.16_spmd, %region_16.17_spmd} | conditional | flops 810287104 | bytes 19925000 | solution.py:94
  253.6 3.6 copy.147
  257.5 3.0 fusion.161
  260.5 3.1 fusion.151
  263.8 1.9 collective-permute-start.5
  265.8 11.3 %collective-permute-done.5 = bf16[512,512]{0,1:T(8,128)(2,1)S(1)} collective-permute-done((bf16[512,512]{0,1:T(8,128)(2,1)S(1)}, bf16[512,512]{0,1:T(8,128)(2,1)S(1)}, u32[]{:S(2)}, u32[]{:S(2)}) %collective-permute-start.5) | collective-permute-done | bytes 524320 | tf_op jit(solution)/shard_map/ppermute | solution.py:12
  277.6 12.2 %collective-permute-start.6 = (bf16[512,512]{0,1:T(8,128)(2,1)S(1)}, bf16[512,512]{0,1:T(8,128)(2,1)S(1)}, u32[]{:S(2)}, u32[]{:S(2)}) collective-permute-start(bf16[512,512]{0,1:T(8,128)(2,1)S(1)} %copy.153), channel_id=1, source_target_pairs={{0,1},{1,2},{2,3},{3,4},{4,5},{5,6},{6,7},{8,9},{9,10},{10,11},{11... | collective-permute-start | bytes 1572872 | tf_op jit(solution)/shard_map/ppermute | solution.py:12
  289.9 7.9 %collective-permute-done.6 = bf16[512,512]{0,1:T(8,128)(2,1)S(1)} collective-permute-done((bf16[512,512]{0,1:T(8,128)(2,1)S(1)}, bf16[512,512]{0,1:T(8,128)(2,1)S(1)}, u32[]{:S(2)}, u32[]{:S(2)}) %collective-permute-start.6) | collective-permute-done | bytes 524320 | tf_op jit(solution)/shard_map/ppermute | solution.py:12
  297.8 3.0 fusion.218
  300.8 3.2 multiply_add_fusion
  305.3 182.2 %while.11 = (s32[]{:T(128)}, f32[2,128,512]{2,1,0:T(8,128)S(1)}, s32[]{:T(128)}, s32[1,24]{1,0:T(1,128)S(1)}, bf16[1,24,128,128]{3,2,1,0:T(8,128)(2,1)}, /*index...) while((s32[]{:T(128)}, f32[2,128,512]{2,1,0:T(8,128)S(1)}, ...), condition=%wide.region_3.4_spmd, body=%wide.region_1.3_spmd.sunk | while | flops 16908316 | bytes 689444 | solution.py:72
  311.2 1.7 fusion.266
  318.7 1.7 fusion.266
  326.3 1.7 fusion.266
  333.9 1.7 fusion.266
  341.4 1.7 fusion.266
  349.0 1.7 fusion.266
  356.6 1.7 fusion.266
  364.1 1.7 fusion.266
  371.7 1.7 fusion.266
  379.3 1.7 fusion.266
  386.8 1.7 fusion.266
  394.4 1.7 fusion.266
  401.9 1.7 fusion.266
  409.5 1.7 fusion.266
  417.1 1.7 fusion.266
  424.6 1.7 fusion.266
  447.3 1.7 fusion.266
  454.9 1.7 fusion.266
  477.6 1.7 fusion.266
  485.2 1.7 fusion.266
  487.6 2.4 fusion.227
  (113 shorter events, 51.8 us)
Async XLA Ops:
  7.2 119.6 %copy-start = (bf16[3,512,512]{2,1,0:T(8,128)(2,1)S(1)}, bf16[3,512,512]{2,1,0:T(8,128)(2,1)}, u32[]{:S(2)}) copy-start(bf16[3,512,512]{2,1,0:T(8,128)(2,1)} %param.34) | copy-start | bytes 4718596
  7.2 119.6 %all-reduce.2.cloned.1.call-start = ((), (), s32[]{:S(2)}) async-start(), calls=%async_computation.2 | async-start | bytes 1048576 | tf_op jit(solution)/shard_map/psum | solution.py:81
  10.0 120.5 %copy-start.3 = (f32[512,512]{1,0:T(8,128)S(1)}, f32[512,512]{1,0:T(8,128)}, u32[]{:S(2)}) copy-start(f32[512,512]{1,0:T(8,128)} %param.37) | copy-start | bytes 3145732
  10.0 120.5 %copy-start.8 = (f32[512]{0:T(512)S(1)}, f32[512]{0:T(512)}, u32[]{:S(2)}) copy-start(f32[512]{0:T(512)} %param.36) | copy-start | bytes 6148
  130.8 15.8 %collective-permute-start = (bf16[512,512]{0,1:T(8,128)(2,1)S(1)}, bf16[512,512]{0,1:T(8,128)(2,1)S(1)}, u32[]{:S(2)}, u32[]{:S(2)}) collective-permute-start(bf16[512,512]{0,1:T(8,128)(2,1)S(1)} %copy.128), channel_id=1, source_target_pairs={{0,1},{1,2},{2,3},{3,4},{4,5},{5,6},{6,7},{8,9},{9,10},{10,11},{11... | collective-permute-start | bytes 1572872 | tf_op jit(solution)/shard_map/ppermute | solution.py:12
  148.0 3.0 copy-start.9
  148.5 17.1 %collective-permute-start.1 = (bf16[512,512]{0,1:T(8,128)(2,1)S(1)}, bf16[512,512]{0,1:T(8,128)(2,1)S(1)}, u32[]{:S(2)}, u32[]{:S(2)}) collective-permute-start(bf16[512,512]{0,1:T(8,128)(2,1)S(1)} %copy.133), channel_id=1, source_target_pairs={{0,1},{1,2},{2,3},{3,4},{4,5},{5,6},{6,7},{8,9},{9,10},{10,11},{11... | collective-permute-start | bytes 1572872 | tf_op jit(solution)/shard_map/ppermute | solution.py:12
  151.9 12.4 %all-to-all-start = ((s32[32,1,1]{2,1,0:T(1,128)}), s32[32,1,1]{2,1,0:T(1,128)S(1)}, u32[]{:S(2)}, u32[]{:S(2)}) async-start(s32[32,1,1]{2,1,0:T(1,128)} %copy.126), calls=%async_computation | async-start | bytes 32768 | tf_op jit(solution)/shard_map/all_to_all | solution.py:58
  166.0 2.8 copy-start.2
  166.2 16.2 %collective-permute-start.2 = (bf16[512,512]{0,1:T(8,128)(2,1)S(1)}, bf16[512,512]{0,1:T(8,128)(2,1)S(1)}, u32[]{:S(2)}, u32[]{:S(2)}) collective-permute-start(bf16[512,512]{0,1:T(8,128)(2,1)S(1)} %copy.137), channel_id=1, source_target_pairs={{0,1},{1,2},{2,3},{3,4},{4,5},{5,6},{6,7},{8,9},{9,10},{10,11},{11... | collective-permute-start | bytes 1572872 | tf_op jit(solution)/shard_map/ppermute | solution.py:12
  176.3 129.0 %all-to-all-start.1 = ((bf16[32,1,128,512]{3,2,1,0:T(8,128)(2,1)}), bf16[32,1,128,512]{3,2,1,0:T(8,128)(2,1)}, u32[]{:S(2)}, u32[]{:S(2)}) async-start(bf16[32,1,128,512]{3,2,1,0:T(8,128)(2,1)} %bitcast_select_fusion), calls=%async_computation.1 | async-start | bytes 8388608 | tf_op jit(solution)/shard_map/all_to_all | solution.py:60
  183.1 16.1 %collective-permute-start.3 = (bf16[512,512]{0,1:T(8,128)(2,1)S(1)}, bf16[512,512]{0,1:T(8,128)(2,1)S(1)}, u32[]{:S(2)}, u32[]{:S(2)}) collective-permute-start(bf16[512,512]{0,1:T(8,128)(2,1)S(1)} %copy.141), channel_id=1, source_target_pairs={{0,1},{1,2},{2,3},{3,4},{4,5},{5,6},{6,7},{8,9},{9,10},{10,11},{11... | collective-permute-start | bytes 1572872 | tf_op jit(solution)/shard_map/ppermute | solution.py:12
  199.7 53.7 %collective-permute-start.4 = (bf16[512,512]{0,1:T(8,128)(2,1)S(1)}, bf16[512,512]{0,1:T(8,128)(2,1)S(1)}, u32[]{:S(2)}, u32[]{:S(2)}) collective-permute-start(bf16[512,512]{0,1:T(8,128)(2,1)S(1)} %copy.145), channel_id=1, source_target_pairs={{0,1},{1,2},{2,3},{3,4},{4,5},{5,6},{6,7},{8,9},{9,10},{10,11},{11... | collective-permute-start | bytes 1572872 | tf_op jit(solution)/shard_map/ppermute | solution.py:12
  263.8 13.2 %collective-permute-start.5 = (bf16[512,512]{0,1:T(8,128)(2,1)S(1)}, bf16[512,512]{0,1:T(8,128)(2,1)S(1)}, u32[]{:S(2)}, u32[]{:S(2)}) collective-permute-start(bf16[512,512]{0,1:T(8,128)(2,1)S(1)} %copy.149), channel_id=1, source_target_pairs={{0,1},{1,2},{2,3},{3,4},{4,5},{5,6},{6,7},{8,9},{9,10},{10,11},{11... | collective-permute-start | bytes 1572872 | tf_op jit(solution)/shard_map/ppermute | solution.py:12
  277.4 12.5 %copy-start.10 = (s32[1,24]{1,0:T(1,128)S(1)}, s32[1,24]{1,0:T(1,128)}, u32[]{:S(2)}) copy-start(s32[1,24]{1,0:T(1,128)} %param.29) | copy-start | bytes 292
  277.6 20.2 %collective-permute-start.6 = (bf16[512,512]{0,1:T(8,128)(2,1)S(1)}, bf16[512,512]{0,1:T(8,128)(2,1)S(1)}, u32[]{:S(2)}, u32[]{:S(2)}) collective-permute-start(bf16[512,512]{0,1:T(8,128)(2,1)S(1)} %copy.153), channel_id=1, source_target_pairs={{0,1},{1,2},{2,3},{3,4},{4,5},{5,6},{6,7},{8,9},{9,10},{10,11},{11... | collective-permute-start | bytes 1572872 | tf_op jit(solution)/shard_map/ppermute | solution.py:12
  304.0 1.4 copy-start.4
  304.0 1.3 copy-start.7
  487.5 2.4 copy-start.1
Sparse Core Ops, SparseCore 0:
  11.8 114.9 all-reduce.1
where the time goes:
time: 500 us; the launch traced here: 497 us
  waiting for transfers between devices  219 us (44%)
  loops' own time  107 us (21%)
  matrix products  62.5 us (12%)
  starting transfers between devices  38.1 us (8%)
  local copies, waits for them, and re-layouts  28 us (6%)
  other arithmetic  26.7 us (5%)
  between operations  15.1 us (3%)
    psum x1, waiting for transfers between devices, shards(): lax.psum(jnp.stack(partial_pool).astype(jnp.bfloat16), 'dom')  117 us
    another operation x1, loops' own time, shards(): totals = lax.fori_loop(0, tile_used[s, 0], add_tile, totals)  107 us
    ppermute x7, waiting for transfers between devices, shifted(): return lax.ppermute(block, axis, route)  96.3 us
    dot_general x24, matrix products, add_tile(): jnp.dot(tile_vals[s, j], source_of(s, j), preferred_element_type=jnp.floa...  41.4 us
    ppermute x7, starting transfers between devices, shifted(): return lax.ppermute(block, axis, route)  25.7 us
    another operation x24, other arithmetic  18.3 us
    dynamic_slice x24, local copies, waits for them, and re-layouts, source_of(): return fetched[owner_dev[s, j], s]  15.4 us
  transfers between devices with their start and end apart: 10, of which 7 were waited for; matrix products, arithmetic and copies ran while one was open for 6% of the time, Pallas kernels for 0%

commit v1 on v0

--- a/solution.py
+++ b/solution.py
@@ -2,6 +2,7 @@
 import jax.numpy as jnp
 from jax import lax
 from jax.sharding import PartitionSpec as P
+from jax.lax import all_gather
 
 BLOCK = 128
 
@@ -78,7 +79,11 @@
     partial_pool = [
         jnp.einsum("nd,nk->dk", features[s], pool_gates, preferred_element_type=jnp.float32)
     ]
-    pooled = lax.psum(jnp.stack(partial_pool).astype(jnp.bfloat16), "dom").astype(jnp.float32)
+    pooled = (
+        all_gather(jnp.stack(partial_pool).astype(jnp.bfloat16), "dom")
+        .sum(axis=0)
+        .astype(jnp.float32)
+    )
     summary = (pooled * (rows_dev * n_dom) ** (-0.5)).astype(jnp.bfloat16)
     in_side = jnp.einsum("gij,tjk->tgik", w_in, summary, preferred_element_type=jnp.float32)
 

time: 500 us -> 483 us (0.966)
  waiting for transfers between devices: 219 us -> 183 us
  local copies, waits for them, and re-layouts: 28 us -> 40.6 us
  other arithmetic: 26.7 us -> 32.3 us
    psum x1 -> x0, waiting for transfers between devices: 117 us -> none  [shards(): lax.psum(jnp.stack(partial_pool).astype(jnp.bfloat16), 'dom')]
    all_gather x0 -> x1, waiting for transfers between devices: none -> 86.1 us  [shards(): all_gather(jnp.stack(partial_pool).astype(jnp.bfloat16), 'dom').sum(axis=0)]
    unnamed x20 -> x25, local copies, waits for them, and re-layouts: 2.69 us -> 16.2 us
    reduce_sum x0 -> x1, other arithmetic: none -> 5.8 us  [shards(): pooled = all_gather(jnp.stack(partial_pool).astype(jnp.bfloat16), 'dom')....]
  transfers between devices with their start and end apart: 10 -> 10, of which waited for: 7 -> 7; matrix products, arithmetic and copies ran while one was open for 6% -> 20% of each run, Pallas kernels for 0% -> 0%
where the time goes in v1:
time: 483 us; the launch traced here: 480 us
  waiting for transfers between devices  183 us (38%)
  loops' own time  109 us (23%)
  matrix products  61.4 us (13%)
  local copies, waits for them, and re-layouts  40.6 us (8%)
  starting transfers between devices  38 us (8%)
  other arithmetic  32.3 us (7%)
  between operations  15.1 us (3%)
    another operation x1, loops' own time, shards(): totals = lax.fori_loop(0, tile_used[s, 0], add_tile, totals)  108 us
    ppermute x7, waiting for transfers between devices, shifted(): return lax.ppermute(block, axis, route)  92.4 us
    all_gather x1, waiting for transfers between devices, shards(): all_gather(jnp.stack(partial_pool).astype(jnp.bfloat16), 'dom').sum(axis=0)  86.1 us
    dot_general x24, matrix products, add_tile(): jnp.dot(tile_vals[s, j], source_of(s, j), preferred_element_type=jnp.floa...  41.3 us
    ppermute x7, starting transfers between devices, shifted(): return lax.ppermute(block, axis, route)  25.4 us
    another operation x24, other arithmetic  17.3 us
    unnamed x25, local copies, waits for them, and re-layouts  16.2 us
    dynamic_slice x24, local copies, waits for them, and re-layouts, source_of(): return fetched[owner_dev[s, j], s]  14.4 us
  transfers between devices with their start and end apart: 10, of which 7 were waited for; matrix products, arithmetic and copies ran while one was open for 20% of the time, Pallas kernels for 0%

profile of v1, /device:TPU:162, one launch (start us, length us, event | category | flops | bytes accessed | tf_op | source)
XLA Modules:
  0.0 479.8 jit_solution(8554582464251334824)
XLA Ops:
  7.2 2.8 fusion.220
  10.7 86.1 %all-gather.3.cloned.1.call-done = bf16[16384,512]{0,1:T(8,128)(2,1)} async-done(((bf16[512,512]{0,1:T(8,128)(2,1)}), bf16[16384,512]{0,1:T(8,128)(2,1)}) %all-gather.3.cloned.1.call-update) | async-done | bytes 16777232 | tf_op jit(solution)/shard_map/all_gather | solution.py:83
  96.9 12.1 %copy.168 = bf16[64,8,32,512]{3,2,1,0:T(8,128)(2,1)S(1)} copy(bf16[64,8,32,512]{3,1,2,0:T(8,128)(2,1)} %bitcast.369) | data formatting | bytes 33554432
  109.0 5.8 %bitcast_reduce_fusion = bf16[512,512]{0,1:T(8,128)(2,1)S(1)} fusion(bf16[64,8,32,512]{3,2,1,0:T(8,128)(2,1)S(1)} %copy.168), kind=kLoop, calls=%fused_computation.230 | loop fusion | flops 8126464 | bytes 17301504 | tf_op jit(solution)/shard_map/reduce_sum | solution.py:84
  114.8 2.7 convolution_bitcast_fusion.8
  117.8 2.6 collective-permute-start
  121.2 6.7 %all-to-all-start = ((s32[32,1,1]{2,1,0:T(1,128)}), s32[32,1,1]{2,1,0:T(1,128)S(1)}, u32[]{:S(2)}, u32[]{:S(2)}) async-start(s32[32,1,1]{2,1,0:T(1,128)} %copy.126), calls=%async_computation | async-start | bytes 32768 | tf_op jit(solution)/shard_map/all_to_all | solution.py:59
  129.2 4.8 %all-to-all-done = s32[32,1,1]{2,1,0:T(1,128)S(1)} async-done(((s32[32,1,1]{2,1,0:T(1,128)}), s32[32,1,1]{2,1,0:T(1,128)S(1)}, u32[]{:S(2)}, u32[]{:S(2)}) %all-to-all-start) | async-done | bytes 160 | tf_op jit(solution)/shard_map/all_to_all | solution.py:59
  135.4 2.8 gather_fusion
  139.9 2.6 collective-permute-start.1
  142.5 4.7 bitcast_select_fusion
  147.1 5.9 %all-to-all-start.1 = ((bf16[32,1,128,512]{3,2,1,0:T(8,128)(2,1)}), bf16[32,1,128,512]{3,2,1,0:T(8,128)(2,1)}, u32[]{:S(2)}, u32[]{:S(2)}) async-start(bf16[32,1,128,512]{3,2,1,0:T(8,128)(2,1)} %bitcast_select_fusion), calls=%async_computation.1 | async-start | bytes 8388608 | tf_op jit(solution)/shard_map/all_to_all | solution.py:61
  153.1 2.4 collective-permute-done.1
  156.3 2.6 collective-permute-start.2
  158.8 13.0 %collective-permute-done.2 = bf16[512,512]{0,1:T(8,128)(2,1)S(1)} collective-permute-done((bf16[512,512]{0,1:T(8,128)(2,1)S(1)}, bf16[512,512]{0,1:T(8,128)(2,1)S(1)}, u32[]{:S(2)}, u32[]{:S(2)}) %collective-permute-start.2) | collective-permute-done | bytes 524320 | tf_op jit(solution)/shard_map/ppermute | solution.py:13
  172.4 1.9 collective-permute-start.3
  174.4 13.2 %collective-permute-done.3 = bf16[512,512]{0,1:T(8,128)(2,1)S(1)} collective-permute-done((bf16[512,512]{0,1:T(8,128)(2,1)S(1)}, bf16[512,512]{0,1:T(8,128)(2,1)S(1)}, u32[]{:S(2)}, u32[]{:S(2)}) %collective-permute-start.3) | collective-permute-done | bytes 524320 | tf_op jit(solution)/shard_map/ppermute | solution.py:13
  188.2 1.9 collective-permute-start.4
  190.2 52.4 %collective-permute-done.4 = bf16[512,512]{0,1:T(8,128)(2,1)S(1)} collective-permute-done((bf16[512,512]{0,1:T(8,128)(2,1)S(1)}, bf16[512,512]{0,1:T(8,128)(2,1)S(1)}, u32[]{:S(2)}, u32[]{:S(2)}) %collective-permute-start.4) | collective-permute-done | bytes 524320 | tf_op jit(solution)/shard_map/ppermute | solution.py:13
  242.7 10.0 %conditional.12 = (bf16[512,512]{1,0:T(8,128)(2,1)S(1)}) conditional(s32[]{:T(128)} %convert_element_type.160, (f32[512,512]{0,1:T(8,128)S(1)}) %tuple.103, (f32[1,3,512,512]{2,3,1,0:T(8,128)}, bf16[3,512,512]{2,1,0:T(8,128)(2,1)}, f32[512,512]{0,1:T(8,128)S(1)}, f32[512]{0:T(512)S(1)}) %tuple.144), branch_computations={%region_15.16_spmd, %region_16.17_spmd} | conditional | flops 810287104 | bytes 19925000 | solution.py:99
  242.7 3.6 copy.147
  246.6 3.0 fusion.161
  249.5 3.1 fusion.151
  252.9 1.9 collective-permute-start.5
  254.9 11.4 %collective-permute-done.5 = bf16[512,512]{0,1:T(8,128)(2,1)} collective-permute-done((bf16[512,512]{0,1:T(8,128)(2,1)S(1)}, bf16[512,512]{0,1:T(8,128)(2,1)}, u32[]{:S(2)}, u32[]{:S(2)}) %collective-permute-start.5) | collective-permute-done | bytes 524320 | tf_op jit(solution)/shard_map/ppermute | solution.py:13
  268.2 12.0 %collective-permute-start.6 = (bf16[512,512]{0,1:T(8,128)(2,1)S(1)}, bf16[512,512]{0,1:T(8,128)(2,1)}, u32[]{:S(2)}, u32[]{:S(2)}) collective-permute-start(bf16[512,512]{0,1:T(8,128)(2,1)S(1)} %copy.153), channel_id=1, source_target_pairs={{0,1},{1,2},{2,3},{3,4},{4,5},{5,6},{6,7},{8,9},{9,10},{10,11},{11... | collective-permute-start | bytes 1572872 | tf_op jit(solution)/shard_map/ppermute | solution.py:13
  280.1 181.4 %while.11 = (s32[]{:T(128)}, f32[2,128,512]{2,1,0:T(8,128)S(1)}, s32[]{:T(128)}, s32[1,24]{1,0:T(1,128)S(1)}, bf16[1,24,128,128]{3,2,1,0:T(8,128)(2,1)}, /*index...) while((s32[]{:T(128)}, f32[2,128,512]{2,1,0:T(8,128)S(1)}, ...), condition=%wide.region_3.4_spmd, body=%wide.region_1.3_spmd.sunk | while | flops 16908316 | bytes 689436 | solution.py:73
  286.0 1.7 fusion.266
  293.5 1.7 fusion.266
  308.6 1.7 fusion.266
  316.1 1.7 fusion.266
  323.6 1.7 fusion.266
  331.2 1.7 fusion.266
  338.7 1.7 fusion.266
  353.7 1.7 fusion.266
  361.3 1.7 fusion.266
  368.8 1.7 fusion.266
  383.9 1.7 fusion.266
  398.9 1.7 fusion.266
  406.5 1.7 fusion.266
  414.0 1.7 fusion.266
  429.1 1.7 fusion.266
  444.1 1.7 fusion.266
  451.7 1.7 fusion.266
  459.2 1.7 fusion.266
  461.7 3.3 fusion.218
  464.9 4.3 multiply_add_fusion
  469.2 2.7 copy.154
  (119 shorter events, 54.2 us)
Async XLA Ops:
  7.2 107.6 %copy-start = (bf16[3,512,512]{2,1,0:T(8,128)(2,1)S(1)}, bf16[3,512,512]{2,1,0:T(8,128)(2,1)}, u32[]{:S(2)}) copy-start(bf16[3,512,512]{2,1,0:T(8,128)(2,1)} %param.34) | copy-start | bytes 4718596
  7.2 3.5 copy-start.11
  7.2 89.7 %all-gather.3.cloned.1.call-start = ((), (), s32[]{:S(2)}) async-start(), calls=%async_computation.2 | async-start | bytes 17301504 | tf_op jit(solution)/shard_map/all_gather | solution.py:83
  114.8 2.7 copy-start.3
  114.8 2.7 copy-start.10
  117.6 17.8 %copy-start.2 = (bf16[1,256,512]{2,1,0:T(8,128)(2,1)S(1)}, bf16[1,256,512]{2,1,0:T(8,128)(2,1)}, u32[]{:S(2)}) copy-start(bf16[1,256,512]{2,1,0:T(8,128)(2,1)} %param.28) | copy-start | bytes 786436
  117.8 20.4 %collective-permute-start = (bf16[512,512]{0,1:T(8,128)(2,1)S(1)}, bf16[512,512]{0,1:T(8,128)(2,1)}, u32[]{:S(2)}, u32[]{:S(2)}) collective-permute-start(bf16[512,512]{0,1:T(8,128)(2,1)S(1)} %copy.128), channel_id=1, source_target_pairs={{0,1},{1,2},{2,3},{3,4},{4,5},{5,6},{6,7},{8,9},{9,10},{10,11},{11... | collective-permute-start | bytes 1572872 | tf_op jit(solution)/shard_map/ppermute | solution.py:13
  121.2 12.8 %all-to-all-start = ((s32[32,1,1]{2,1,0:T(1,128)}), s32[32,1,1]{2,1,0:T(1,128)S(1)}, u32[]{:S(2)}, u32[]{:S(2)}) async-start(s32[32,1,1]{2,1,0:T(1,128)} %copy.126), calls=%async_computation | async-start | bytes 32768 | tf_op jit(solution)/shard_map/all_to_all | solution.py:59
  135.4 2.9 copy-start.4
  139.9 15.6 %collective-permute-start.1 = (bf16[512,512]{0,1:T(8,128)(2,1)S(1)}, bf16[512,512]{0,1:T(8,128)(2,1)S(1)}, u32[]{:S(2)}, u32[]{:S(2)}) collective-permute-start(bf16[512,512]{0,1:T(8,128)(2,1)S(1)} %copy.133), channel_id=1, source_target_pairs={{0,1},{1,2},{2,3},{3,4},{4,5},{5,6},{6,7},{8,9},{9,10},{10,11},{11... | collective-permute-start | bytes 1572872 | tf_op jit(solution)/shard_map/ppermute | solution.py:13
  147.1 133.0 %all-to-all-start.1 = ((bf16[32,1,128,512]{3,2,1,0:T(8,128)(2,1)}), bf16[32,1,128,512]{3,2,1,0:T(8,128)(2,1)}, u32[]{:S(2)}, u32[]{:S(2)}) async-start(bf16[32,1,128,512]{3,2,1,0:T(8,128)(2,1)} %bitcast_select_fusion), calls=%async_computation.1 | async-start | bytes 8388608 | tf_op jit(solution)/shard_map/all_to_all | solution.py:61
  156.3 15.6 %collective-permute-start.2 = (bf16[512,512]{0,1:T(8,128)(2,1)S(1)}, bf16[512,512]{0,1:T(8,128)(2,1)S(1)}, u32[]{:S(2)}, u32[]{:S(2)}) collective-permute-start(bf16[512,512]{0,1:T(8,128)(2,1)S(1)} %copy.137), channel_id=1, source_target_pairs={{0,1},{1,2},{2,3},{3,4},{4,5},{5,6},{6,7},{8,9},{9,10},{10,11},{11... | collective-permute-start | bytes 1572872 | tf_op jit(solution)/shard_map/ppermute | solution.py:13
  172.4 15.2 %collective-permute-start.3 = (bf16[512,512]{0,1:T(8,128)(2,1)S(1)}, bf16[512,512]{0,1:T(8,128)(2,1)S(1)}, u32[]{:S(2)}, u32[]{:S(2)}) collective-permute-start(bf16[512,512]{0,1:T(8,128)(2,1)S(1)} %copy.141), channel_id=1, source_target_pairs={{0,1},{1,2},{2,3},{3,4},{4,5},{5,6},{6,7},{8,9},{9,10},{10,11},{11... | collective-permute-start | bytes 1572872 | tf_op jit(solution)/shard_map/ppermute | solution.py:13
  188.2 54.3 %collective-permute-start.4 = (bf16[512,512]{0,1:T(8,128)(2,1)S(1)}, bf16[512,512]{0,1:T(8,128)(2,1)S(1)}, u32[]{:S(2)}, u32[]{:S(2)}) collective-permute-start(bf16[512,512]{0,1:T(8,128)(2,1)S(1)} %copy.145), channel_id=1, source_target_pairs={{0,1},{1,2},{2,3},{3,4},{4,5},{5,6},{6,7},{8,9},{9,10},{10,11},{11... | collective-permute-start | bytes 1572872 | tf_op jit(solution)/shard_map/ppermute | solution.py:13
  252.7 2.2 copy-start.12
  252.9 13.4 %collective-permute-start.5 = (bf16[512,512]{0,1:T(8,128)(2,1)S(1)}, bf16[512,512]{0,1:T(8,128)(2,1)}, u32[]{:S(2)}, u32[]{:S(2)}) collective-permute-start(bf16[512,512]{0,1:T(8,128)(2,1)S(1)} %copy.149), channel_id=1, source_target_pairs={{0,1},{1,2},{2,3},{3,4},{4,5},{5,6},{6,7},{8,9},{9,10},{10,11},{11... | collective-permute-start | bytes 1572872 | tf_op jit(solution)/shard_map/ppermute | solution.py:13
  267.5 12.7 %copy-start.8 = (s32[3]{0:T(128)S(1)}, s32[3]{0:T(128)}, u32[]{:S(2)}) copy-start(s32[3]{0:T(128)} %constant.92.clone.1) | copy-start | bytes 40
  268.2 193.5 %collective-permute-start.6 = (bf16[512,512]{0,1:T(8,128)(2,1)S(1)}, bf16[512,512]{0,1:T(8,128)(2,1)}, u32[]{:S(2)}, u32[]{:S(2)}) collective-permute-start(bf16[512,512]{0,1:T(8,128)(2,1)S(1)} %copy.153), channel_id=1, source_target_pairs={{0,1},{1,2},{2,3},{3,4},{4,5},{5,6},{6,7},{8,9},{9,10},{10,11},{11... | collective-permute-start | bytes 1572872 | tf_op jit(solution)/shard_map/ppermute | solution.py:13
  461.6 3.3 copy-start.9
  469.2 2.7 copy-start.5
  469.2 3.7 copy-start.1
Sparse Core Ops, SparseCore 0:
  11.0 85.7 all-gather.2
